TPU v7x, 32 devices: a whole 2x2x4 slice. The times are simulated.
32 devices in a mesh: dp: 4 (over y, x), expert: 8 (over z, core).
Axes of the slice: x: 2, y: 2, z: 4, core: 2. Of those that a mesh axis runs over, the one named last changes fastest.
Arguments:
- tokens: bfloat16 [2, 2048, 4096], P(None, ('dp', 'expert')), may hold values from -64 to 64
- expert_of: int32 [2, 2048], P(None, ('dp', 'expert')), may hold values from 0 to 3, as said below
- w_gate: bfloat16 [8, 4096, 3584], P('expert', None, 'dp'), may hold values from -0.09375 to 0.09375
- w_up: bfloat16 [8, 4096, 3584], P('expert', None, 'dp'), may hold values from -0.09375 to 0.09375
- w_down: bfloat16 [8, 3584, 4096], P('expert', 'dp'), may hold values from -1 to 1
Outputs:
- out: bfloat16 [2, 2048, 4096], P(None, ('dp', 'expert'))
- next_scale: float32 [4], replicated
Inputs may be any that keep to these rules, and one draw needn't show every extreme that they name: `expert_of`: in each microbatch the 64 tokens of one device name each expert at most 18 times, and one expert, the same for all devices of that microbatch, exactly 18 times.
All inputs are finite; a program needn't handle non-finite values.
Results may differ from a plain program's by a relative error of at most 0.012.
Values may be sent and summed in bfloat16 or wider, within the bound.
A program may use at most 128 MiB of HBM per device.

v0:
```python
import jax
import jax.numpy as jnp
from jax import lax
from jax.sharding import PartitionSpec as P

SPAN = 2


clip_target = 2.0


def body(tokens, expert_of, w_gate, w_up, w_down):
    micro_count = tokens.shape[0]
    tok_rows = tokens.shape[1]
    model_width = tokens.shape[2]
    expert_size = lax.axis_size("expert")
    expert_count = expert_size // SPAN
    capacity = max(2, 9 * tok_rows // (8 * expert_count))
    my_expert = lax.axis_index("expert") // SPAN
    gate_local = w_gate[0]
    up_local = w_up[0]
    down_local = w_down[0]
    slot_range = jnp.arange(expert_count * capacity, dtype=jnp.int32)
    expert_range = jnp.arange(expert_count, dtype=jnp.int32)
    clip_scale = jnp.ones((expert_count,), jnp.float32)
    results = []
    for micro_idx in range(micro_count):
        token_ids = expert_of[micro_idx]
        onehot_ids = (token_ids[:, None] == expert_range[None, :]).astype(jnp.int32)
        earlier = jnp.cumsum(onehot_ids, axis=0) - onehot_ids
        slot_of = jnp.sum(earlier * onehot_ids, axis=1)
        position = token_ids * capacity + slot_of
        placing = (position[None, :] == slot_range[:, None]).astype(jnp.bfloat16)
        tokens_now = tokens[micro_idx]
        packed = jnp.dot(placing, tokens_now, preferred_element_type=jnp.float32).astype(
            jnp.bfloat16
        )
        packed = packed.reshape(expert_count, capacity, model_width)
        factor = clip_scale[my_expert]
        sending_all = jnp.repeat(packed, SPAN, axis=0)
        arrived = lax.all_to_all(sending_all, "expert", split_axis=0, concat_axis=0, tiled=True)
        flat_rows = arrived.reshape(expert_size * capacity, model_width)
        rows_in = lax.all_gather(flat_rows, "dp", axis=0, tiled=True)
        rows_in = (factor * rows_in.astype(jnp.float32)).astype(jnp.bfloat16)
        gate_vals = jnp.dot(rows_in, gate_local, preferred_element_type=jnp.float32)
        up_vals = jnp.dot(rows_in, up_local, preferred_element_type=jnp.float32)
        hidden = (jax.nn.silu(gate_vals) * up_vals).astype(jnp.bfloat16)
        summed = lax.psum_scatter(
            jnp.dot(hidden, down_local, preferred_element_type=jnp.float32).astype(jnp.bfloat16),
            "dp",
            scatter_dimension=0,
            tiled=True,
        )
        halves = summed.reshape(expert_size, capacity, model_width)
        returned = lax.all_to_all(halves, "expert", split_axis=0, concat_axis=0, tiled=True)
        returned = lax.optimization_barrier(returned)
        joined = jnp.sum(
            returned.reshape(expert_count, SPAN, capacity, model_width).astype(jnp.float32), axis=1
        )
        token_out = jnp.take(joined.reshape(expert_count * capacity, model_width), position, axis=0)
        results.append(token_out.astype(jnp.bfloat16))
        squares = jnp.sum(token_out * token_out, axis=1)
        onehot_float = onehot_ids.astype(jnp.float32)
        counts_local = jnp.sum(onehot_float, axis=0)
        square_local = jnp.dot(squares[None, :], onehot_float, precision=lax.Precision.HIGHEST)[0]
        counts, square_sums = lax.psum((counts_local, square_local), ("dp", "expert"))
        clip_scale = jnp.minimum(
            1.0,
            clip_target / jnp.sqrt((square_sums + model_width) / (model_width * (counts + 1.0))),
        )
    return (jnp.stack(results), clip_scale)


def solution(mesh):
    return jax.shard_map(
        body,
        mesh=mesh,
        in_specs=(
            P(None, ("dp", "expert"), None),
            P(None, ("dp", "expert")),
            P("expert", None, "dp"),
            P("expert", None, "dp"),
            P("expert", "dp", None),
        ),
        out_specs=(P(None, ("dp", "expert"), None), P()),
        check_vma=False,
    )
```

profile of v0, /device:TPU:0, one launch (start us, length us, event | category | flops | bytes accessed | tf_op | source)
XLA Modules:
  0.0 470.1 jit_solution(3594108372174720230)
XLA Ops:
  7.2 0.7 slice_bitcast_fusion.1
  8.0 0.1 reduce_window_sum.17
  8.1 0.2 fusion.39
  8.2 0.8 fusion.48
  9.0 1.3 convolution_convert_fusion.1
  10.4 0.2 reshape.57
  10.6 0.2 broadcast_in_dim.13
  10.7 43.9 %all_to_all.20 = bf16[8,18,4096]{2,1,0:T(8,128)(2,1)S(1)} all-to-all(bf16[8,18,4096]{2,1,0:T(8,128)(2,1)S(1)} %bitcast.79), channel_id=1, replica_groups=mesh['dp'=4,'expert'=8] {'expert'}, dimensions={0} | all-to-all | bytes 2359296 | tf_op jit(solution)/shard_map/all_to_all | solution.py:41
  54.7 1.2 reshape.59
  56.0 56.0 %all-gather.3.cloned.1.call-done = bf16[576,4096]{1,0:T(8,128)(2,1)} async-done(((bf16[144,4096]{1,0:T(8,128)(2,1)}), bf16[576,4096]{1,0:T(8,128)(2,1)}) %all-gather.3.cloned.1.call-update) | async-done | bytes 4718608 | tf_op jit(solution)/shard_map/all_gather | solution.py:43
  112.0 10.7 %fusion.10 = f32[576,896]{1,0:T(8,128)S(1)} fusion(bf16[576,4096]{1,0:T(8,128)(2,1)} %all-gather.3.cloned.1.call-done, bf16[1,4096,896]{2,1,0:T(8,128)(2,1)} %param.9), kind=kOutput, calls=%fused_computation.13 | convolution fusion | flops 4227858432 | bytes 14123008 | tf_op jit(solution)/shard_map/dot_general | solution.py:45
  122.7 17.5 %fusion.12 = bf16[576,4096]{1,0:T(8,128)(2,1)} fusion(bf16[1,896,4096]{2,1,0:T(8,128)(2,1)} %param.11, f32[576,896]{1,0:T(8,128)S(1)} %fusion.10, bf16[576,4096]{1,0:T(8,128)(2,1)} %all-gather.3.cloned.1.call-done, bf16[1,4096,896]{2,1,0:T(8,128)(2,1)} %param.10), kind=kOutput, calls=%fused_computation.15 | convolution fusion | flops 8461172736 | bytes 26181632 | tf_op jit(solution)/shard_map/dot_general | solution.py:49
  140.4 0.2 fusion.34
  140.6 0.2 copy-done.1
  140.9 0.6 copy-done
  141.4 0.3 convolution_convert_fusion
  141.7 0.2 reshape.62
  141.9 0.2 broadcast_in_dim.14
  142.1 42.2 %all_to_all.21 = bf16[8,18,4096]{2,1,0:T(8,128)(2,1)S(1)} all-to-all(bf16[8,18,4096]{2,1,0:T(8,128)(2,1)S(1)} %bitcast.80), channel_id=1, replica_groups=mesh['dp'=4,'expert'=8] {'expert'}, dimensions={0} | all-to-all | bytes 2359296 | tf_op jit(solution)/shard_map/all_to_all | solution.py:41
  184.3 1.2 reshape.64
  185.5 11.8 %reduce-scatter.3.cloned.1.call-done = bf16[144,4096]{1,0:T(8,128)(2,1)} async-done(((bf16[576,4096]{1,0:T(8,128)(2,1)}), bf16[144,4096]{1,0:T(8,128)(2,1)}) %reduce-scatter.3.cloned.1.call-update) | async-done | bytes 1179664 | tf_op jit(solution)/shard_map/reduce_scatter | solution.py:48
  197.3 2.4 reshape.60
  199.8 4.6 all-to-all-start.1
  204.6 37.6 %all-to-all-done.1 = bf16[8,18,4096]{2,1,0:T(8,128)(2,1)S(1)} async-done(((bf16[8,18,4096]{2,1,0:T(8,128)(2,1)}), bf16[8,18,4096]{2,1,0:T(8,128)(2,1)S(1)}, u32[]{:S(2)}, u32[]{:S(2)}) %all-to-all-start.1) | async-done | bytes 1179680 | tf_op jit(solution)/shard_map/all_to_all | solution.py:55
  242.2 1.4 convert_reduce_fusion.1
  243.6 1.6 reshape.61
  245.2 0.9 gather_fusion
  246.1 0.3 multiply_reduce_fusion.1
  246.4 0.2 convolution_bitcast_fusion.1
  246.6 37.3 %all-reduce.1 = (f32[4]{0:T(128)S(1)}, f32[4]{0:T(128)S(1)}) all-reduce(f32[4]{0:T(128)S(1)} %convert_reduce_fusion.3, f32[4]{0:T(128)S(1)} %convolution_bitcast_fusion.1), channel_id=1, replica_groups=mesh['dp'=4,'expert'=8] {'dp','expert'}, use_global_device_ids=true, to_apply=%region_7.9 | all-reduce | flops 8 | bytes 64 | tf_op jit(solution)/shard_map/psum | solution.py:66
  283.9 0.6 dynamic_slice.3
  284.5 12.6 %fusion.8 = f32[576,896]{1,0:T(8,128)S(1)} fusion(bf16[1,4096,896]{2,1,0:T(8,128)(2,1)} %param.9, bf16[576,4096]{1,0:T(8,128)(2,1)} %all-gather.5.cloned.1.call-done, f32[]{:T(128)} %bitcast.13), kind=kOutput, calls=%fused_computation.11 | convolution fusion | flops 4234936320 | bytes 14123012 | tf_op jit(solution)/shard_map/dot_general | solution.py:45
  297.1 8.9 %multiply_convert_fusion.3 = bf16[576,896]{1,0:T(8,128)(2,1)S(1)} fusion(f32[576,896]{1,0:T(8,128)S(1)} %fusion.8, bf16[1,4096,896]{2,1,0:T(8,128)(2,1)} %param.10, bf16[576,4096]{1,0:T(8,128)(2,1)S(1)} %copy-done.2, f32[]{:T(128)} %bitcast.13), kind=kOutput, calls=%fused_computation.21 | convolution fusion | flops 4238032896 | bytes 15155204 | tf_op jit(solution)/shard_map/dot_general | solution.py:46
  306.0 9.8 %fusion.15 = bf16[576,4096]{1,0:T(8,128)(2,1)} fusion(bf16[576,896]{1,0:T(8,128)(2,1)S(1)} %multiply_convert_fusion.3, bf16[1,896,4096]{2,1,0:T(8,128)(2,1)} %param.11), kind=kOutput, calls=%fused_computation.16 | convolution fusion | flops 4230217728 | bytes 13090816 | tf_op jit(solution)/shard_map/dot_general | solution.py:49
  315.8 58.3 %reduce-scatter.5.cloned.1.call-done = bf16[144,4096]{1,0:T(8,128)(2,1)} async-done(((bf16[576,4096]{1,0:T(8,128)(2,1)}), bf16[144,4096]{1,0:T(8,128)(2,1)}) %reduce-scatter.5.cloned.1.call-update) | async-done | bytes 1179664 | tf_op jit(solution)/shard_map/reduce_scatter | solution.py:48
  374.1 2.4 reshape.65
  376.5 4.6 all-to-all-start.3
  381.2 0.1 fusion.25
  381.3 37.7 %all-to-all-done.3 = bf16[8,18,4096]{2,1,0:T(8,128)(2,1)} async-done(((bf16[8,18,4096]{2,1,0:T(8,128)(2,1)}), bf16[8,18,4096]{2,1,0:T(8,128)(2,1)}, u32[]{:S(2)}, u32[]{:S(2)}) %all-to-all-start.3) | async-done | bytes 1179680 | tf_op jit(solution)/shard_map/all_to_all | solution.py:55
  419.0 3.0 convert_reduce_fusion
  422.0 1.6 reshape.66
  423.5 0.9 gather_fusion.1
  424.5 0.3 multiply_reduce_fusion
  424.8 0.2 convolution_bitcast_fusion
  425.0 0.1 fusion.26
  425.1 36.9 %all-reduce = (f32[4]{0:T(128)S(1)}, f32[4]{0:T(128)S(1)}) all-reduce(f32[4]{0:T(128)S(1)} %convert_reduce_fusion.2, f32[4]{0:T(128)S(1)} %convolution_bitcast_fusion), channel_id=1, replica_groups=mesh['dp'=4,'expert'=8] {'dp','expert'}, use_global_device_ids=true, to_apply=%region_15.17 | all-reduce | flops 8 | bytes 64 | tf_op jit(solution)/shard_map/psum | solution.py:66
  462.0 0.5 multiply_minimum_fusion
  462.5 1.1 pad_maximum_fusion
  (23 shorter events, 0.7 us)
Async XLA Ops:
  7.2 104.8 %all-gather.3.cloned.1.call-start = ((), (), s32[]{:S(2)}) async-start(), calls=%async_computation.6 | async-start | bytes 5898240 | tf_op jit(solution)/shard_map/all_gather | solution.py:43
  55.9 141.4 %reduce-scatter.3.cloned.1.call-start = ((), (), s32[]{:S(2)}) async-start(), calls=%async_computation.7 | async-start | bytes 5898240 | tf_op jit(solution)/shard_map/reduce_scatter | solution.py:48
  140.2 0.7 copy-start.1
  140.2 1.2 copy-start
  140.2 144.3 %all-gather.5.cloned.1.call-start = ((), (), s32[]{:S(2)}) async-start(), calls=%async_computation.8 | async-start | bytes 5898240 | tf_op jit(solution)/shard_map/all_gather | solution.py:43
  199.8 42.4 %all-to-all-start.1 = ((bf16[8,18,4096]{2,1,0:T(8,128)(2,1)}), bf16[8,18,4096]{2,1,0:T(8,128)(2,1)S(1)}, u32[]{:S(2)}, u32[]{:S(2)}) async-start(bf16[8,18,4096]{2,1,0:T(8,128)(2,1)} %reshape.60), calls=%async_computation.2 | async-start | bytes 3145728 | tf_op jit(solution)/shard_map/all_to_all | solution.py:55
  204.4 169.7 %reduce-scatter.5.cloned.1.call-start = ((), (), s32[]{:S(2)}) async-start(), calls=%async_computation.9 | async-start | bytes 5898240 | tf_op jit(solution)/shard_map/reduce_scatter | solution.py:48
  284.5 12.6 %copy-start.2 = (bf16[576,4096]{1,0:T(8,128)(2,1)S(1)}, bf16[576,4096]{1,0:T(8,128)(2,1)}, u32[]{:S(2)}) copy-start(bf16[576,4096]{1,0:T(8,128)(2,1)} %all-gather.5.cloned.1.call-done) | copy-start | bytes 14155780
  376.5 42.5 %all-to-all-start.3 = ((bf16[8,18,4096]{2,1,0:T(8,128)(2,1)}), bf16[8,18,4096]{2,1,0:T(8,128)(2,1)}, u32[]{:S(2)}, u32[]{:S(2)}) async-start(bf16[8,18,4096]{2,1,0:T(8,128)(2,1)} %reshape.65), calls=%async_computation.5 | async-start | bytes 3145728 | tf_op jit(solution)/shard_map/all_to_all | solution.py:55
Sparse Core Ops, SparseCore 0:
  56.1 55.8 all-gather.2
  140.3 56.9 reduce-scatter.2
  199.2 57.4 all-gather.4
  315.9 58.1 reduce-scatter.4
where the time goes:
time: 471 us; the launch traced here: 470 us
  waiting for transfers between devices  201 us (43%)
  blocking collectives  160 us (34%)
  matrix products  61.5 us (13%)
  local copies, waits for them, and re-layouts  15 us (3%)
  between operations  13.9 us (3%)
  starting transfers between devices  9.35 us (2%)
  other arithmetic  8.55 us (2%)
    all_to_all x2, blocking collectives, body(): lax.all_to_all(sending_all, 'expert', split_axis=0, concat_axis=0, tiled=...  86.1 us
    all_to_all x2, waiting for transfers between devices, body(): lax.all_to_all(halves, 'expert', split_axis=0, concat_axis=0, tiled=True)  75.3 us
    psum x2, blocking collectives, body(): lax.psum((counts_local, square_local), ('dp', 'expert'))  74.2 us
    reduce_scatter x2, waiting for transfers between devices, body(): lax.psum_scatter(jnp.dot(hidden, down_local, preferred_element_type=jnp.f...  70.1 us
    all_gather x2, waiting for transfers between devices, body(): rows_in = lax.all_gather(flat_rows, 'dp', axis=0, tiled=True)  56 us
    dot_general x2, matrix products, body(): jnp.dot(hidden, down_local, preferred_element_type=jnp.float32)  27.3 us
    dot_general x2, matrix products, body(): gate_vals = jnp.dot(rows_in, gate_local, preferred_element_type=jnp.float32)  23.3 us
  transfers between devices with their start and end apart: 6, of which 5 were waited for; matrix products, arithmetic and copies ran while one was open for 2% of the time, Pallas kernels for 0%

commit v1 on v0

--- a/solution.py
+++ b/solution.py
@@ -1,6 +1,10 @@
+import functools
+
 import jax
 import jax.numpy as jnp
 from jax import lax
+from jax.experimental import pallas as pl
+from jax.experimental.pallas import tpu as pltpu
 from jax.sharding import PartitionSpec as P
 
 SPAN = 2
@@ -71,9 +75,515 @@
     return (jnp.stack(results), clip_scale)
 
 
+MESH = pl.DeviceIdType.MESH
+F32 = jnp.float32
+BF16 = jnp.bfloat16
+ROWS = 16
+CHUNKS = 4
+LANES = 128
+
+
+def mm(a, b):
+    return jnp.dot(a, b, preferred_element_type=F32)
+
+
+def iota(shape, dim):
+    return lax.broadcasted_iota(jnp.int32, shape, dim)
+
+
+def kernel(
+    sizes,
+    tok_ref, idr_ref, idc_ref, wg_hbm, wu_hbm, wd_hbm,
+    out_ref, scale_ref,
+    wg, wu, wd, pk, xg, xr, hid, g1, u1, sb, rb, own, rd, ra, rc, fr, f2, ret,
+    cst, sqst, fst,
+    wsem, ssem, rsem, lsem, csend, crecv, qsend, qrecv, fsend, frecv,
+):
+    micro, toks, width, ff, nd, ne, cap = sizes
+    extra = cap - ROWS
+    pieces = ROWS // extra
+    piece = width // pieces
+    experts = ne // SPAN
+    blocks = experts * SPAN
+    main_rows = blocks * ROWS
+    extra_rows = blocks * extra
+    half = width // 2
+    ch = half // CHUNKS
+    pair_w = 2 * ch
+    pair_piece = pair_w // pieces
+    ndev = nd * ne
+
+    d = lax.axis_index("dp")
+    ex = lax.axis_index("expert")
+    z = ex // 2
+    c = ex % 2
+    dx = d + 1 - 2 * (d % 2)
+    dy = d + 2 - 4 * (d // 2)
+    dd = 3 - d
+    sib = z * 2 + 1 - c
+    flat = d * ne + ex
+    flat_q = d * 2 + c
+
+    weights = [
+        pltpu.make_async_copy(wg_hbm.at[0], wg, wsem.at[0]),
+        pltpu.make_async_copy(wu_hbm.at[0], wu, wsem.at[1]),
+        pltpu.make_async_copy(wd_hbm.at[0], wd, wsem.at[2]),
+    ]
+    for copy in weights:
+        copy.start()
+
+    barrier = pltpu.get_barrier_semaphore()
+
+    def greet(t, carry):
+        to = (flat + t) % ndev
+        pl.semaphore_signal(barrier, inc=1, device_id=(to // ne, to % ne), device_id_type=MESH)
+        return carry
+
+    lax.fori_loop(1, ndev, greet, 0)
+
+    slots = experts * ROWS
+    place = []
+    counts = []
+    for m in range(micro):
+        idr = idr_ref[m]
+        idc = idc_ref[m]
+        before_r = (idc == idr) & (iota((toks, toks), 0) < iota((toks, toks), 1))
+        slot_r = jnp.sum(before_r.astype(F32), axis=0, keepdims=True).astype(jnp.int32)
+        before_c = (idc == idr) & (iota((toks, toks), 1) < iota((toks, toks), 0))
+        slot_c = jnp.sum(before_c.astype(F32), axis=1, keepdims=True).astype(jnp.int32)
+        place.append((idr, idc, slot_r, slot_c))
+        hit = (idc == iota((toks, LANES), 1)).astype(F32)
+        counts.append(jnp.sum(hit, axis=0, keepdims=True))
+    row8 = iota((8, LANES), 0)
+    lane8 = iota((8, LANES), 1)
+    count_tile = jnp.zeros((8, LANES), F32)
+    for m in range(micro):
+        count_tile = jnp.where(row8 == m, counts[m], count_tile)
+    cst[flat] = count_tile
+
+    def pack(m):
+        idr, _, slot_r, _ = place[m]
+        row = iota((slots, toks), 0)
+        pick = ((idr == row // ROWS) & (slot_r == row % ROWS)).astype(F32).astype(BF16)
+        pick_x = ((idr == row // ROWS) & (slot_r == ROWS + (row % ROWS) // pieces)).astype(F32).astype(BF16)
+        rowp = iota((slots, piece), 0) % pieces
+        tail = jnp.zeros((slots, piece), F32)
+        for p in range(pieces):
+            cols = tok_ref[m, :, p * piece:(p + 1) * piece]
+            pk[m, :, :, p * piece:(p + 1) * piece] = mm(pick, cols).astype(BF16).reshape(experts, ROWS, piece)
+            tail = jnp.where(rowp == p, mm(pick_x, cols), tail)
+        pk[m, :, :, width:] = tail.astype(BF16).reshape(experts, ROWS, piece)
+
+    sends = []
+    index = {}
+
+    def sem_of(key):
+        return index.setdefault(key, len(index))
+
+    def remote(key, src, dst, dev):
+        i = sem_of(key)
+        copy = pltpu.make_async_remote_copy(
+            src_ref=src, dst_ref=dst, send_sem=ssem.at[i], recv_sem=rsem.at[i],
+            device_id=dev, device_id_type=MESH,
+        )
+        copy.start()
+        sends.append((key, copy))
+        return copy
+
+    def arrived(key, dst):
+        i = sem_of(key)
+        pltpu.make_async_remote_copy(
+            src_ref=dst, dst_ref=dst, send_sem=ssem.at[i], recv_sem=rsem.at[i],
+            device_id=(d, sib), device_id_type=MESH,
+        ).wait_recv()
+
+    def wait_sent(match):
+        left = []
+        for key, copy in sends:
+            if match(key):
+                copy.wait_send()
+            else:
+                left.append((key, copy))
+        sends[:] = left
+
+    locals_ = {}
+
+    def local(key, src, dst):
+        i = len(locals_)
+        copy = pltpu.make_async_copy(src, dst, lsem.at[i])
+        copy.start()
+        locals_[key] = copy
+
+    def zof(t):
+        return (z + experts - t) % experts
+
+    def dispatch(m):
+        local(("z", m), pk.at[m, z], xg.at[m, d, c * experts + z])
+        for t in range(1, experts):
+            to = (z + t) % experts
+            remote(("z", m, t), pk.at[m, to], xg.at[m, d, c * experts + z], (d, to * 2 + c))
+
+    def to_sibling(kind, m, t, slot):
+        remote(("s" + kind, m, t), slot, slot, (d, sib))
+
+    def gather_own(m, t):
+        slot = xg.at[m, d, c * experts + zof(t)]
+        if t == 0:
+            locals_[("z", m)].wait()
+        else:
+            arrived(("z", m, t), slot)
+        remote(("gx", m, t), slot, slot, (dx, ex))
+        remote(("gy", m, t), slot, slot, (dy, ex))
+        to_sibling("o", m, t, slot)
+
+    def gather_xy(m, t):
+        slot = xg.at[m, dx, c * experts + zof(t)]
+        arrived(("gx", m, t), slot)
+        if t < experts // 2:
+            remote(("gd", m, t), slot, slot, (dy, ex))
+        to_sibling("x", m, t, slot)
+        slot = xg.at[m, dy, c * experts + zof(t)]
+        arrived(("gy", m, t), slot)
+        if t >= experts // 2:
+            remote(("gd", m, t), slot, slot, (dx, ex))
+        to_sibling("y", m, t, slot)
+
+    def gather_diag(m, t):
+        slot = xg.at[m, dd, c * experts + zof(t)]
+        arrived(("gd", m, t), slot)
+        to_sibling("d", m, t, slot)
+
+    def gather_end(m):
+        for kind, chip in (("o", d), ("x", dx), ("y", dy), ("d", dd)):
+            for t in range(experts):
+                arrived(("s" + kind, m, t), xg.at[m, chip, (1 - c) * experts + zof(t)])
+
+    allm = nd * main_rows
+    allx = nd * extra_rows
+
+    def spread(m):
+        def one(p, carry):
+            row = iota((allx, allm), 0)
+            want = (row // extra) * ROWS + (row % extra) * pieces + p
+            pick = (iota((allx, allm), 1) == want).astype(F32).astype(BF16)
+            tails = xg[m, :, :, :, width:].reshape(allm, piece)
+            xr[:, pl.ds(pl.multiple_of(p * piece, piece), piece)] = mm(pick, tails).astype(BF16)
+            return carry
+
+        lax.fori_loop(0, pieces, one, 0)
+
+    def gate_up(m, low, high):
+        def one(n, carry):
+            cols = pl.ds(pl.multiple_of(n * LANES, LANES), LANES)
+            rows = jnp.concatenate([xg[m, :, :, :, :width].reshape(allm, width), xr[...]], axis=0)
+            w = jnp.concatenate([wg[:, cols], wu[:, cols]], axis=1)
+            both = mm(rows, w)
+            gate = both[:, :LANES]
+            up = both[:, LANES:]
+            if m == 0:
+                hid[:, cols] = (gate / (1.0 + jnp.exp(-gate)) * up).astype(BF16)
+            else:
+                g1[:, cols] = gate
+                u1[:, cols] = up
+            return carry
+
+        lax.fori_loop(low, high, one, 0)
+
+    def scaled_hidden(scale):
+        def one(n, carry):
+            cols = pl.ds(pl.multiple_of(n * LANES, LANES), LANES)
+            gate = g1[:, cols] * scale
+            up = u1[:, cols] * scale
+            hid[:, cols] = (gate / (1.0 + jnp.exp(-gate)) * up).astype(BF16)
+            return carry
+
+        lax.fori_loop(0, ff // LANES, one, 0)
+
+    def neighbours(j):
+        return (dx, dy) if j % 2 == 0 else (dy, dx)
+
+    def down(side, j):
+        col = pl.multiple_of(side * half + j * ch, ch)
+        return mm(hid[...], wd[:, pl.ds(col, ch)])
+
+    def step_a(m, j):
+        if m > 0:
+            wait_sent(lambda key: key == ("rs", m - 1, j))
+        sb[j] = down(1 - c, j).astype(BF16)
+        remote(("rs", m, j), sb.at[j], rb.at[m, j], (d, sib))
+
+    def step_b(m, j):
+        mine = down(c, j)
+        if m > 0:
+            wait_sent(lambda key: key[0] in ("rd", "ra", "rc") and key[1:] == (m - 1, j))
+        arrived(("rs", m, j), rb.at[m, j])
+        both = (mine + rb[m, j].astype(F32)).astype(BF16)
+        for k in range(nd):
+            own[j, k, :main_rows] = both[k * main_rows:(k + 1) * main_rows]
+            own[j, k, main_rows:] = both[allm + k * extra_rows:allm + (k + 1) * extra_rows]
+        first, _ = neighbours(j)
+        remote(("rd", m, j), own.at[j, dd], rd.at[m, j], (first, ex))
+        remote(("ra", m, j), own.at[j, first], ra.at[m, j], (first, ex))
+
+    def step_c(m, j):
+        _, second = neighbours(j)
+        arrived(("rd", m, j), rd.at[m, j])
+        own[j, second] = (own[j, second].astype(F32) + rd[m, j].astype(F32)).astype(BF16)
+        remote(("rc", m, j), own.at[j, second], rc.at[m, j], (second, ex))
+
+    def step_d(m, j):
+        arrived(("ra", m, j), ra.at[m, j])
+        arrived(("rc", m, j), rc.at[m, j])
+        total = own[j, d].astype(F32) + ra[m, j].astype(F32) + rc[m, j].astype(F32)
+        at = (j % 2) * ch
+        pair = j // 2
+        low = total.astype(BF16)
+        f2[m, pair, :, :, at:at + ch] = low[:main_rows].reshape(blocks, ROWS, ch)
+        fr[:, at:at + ch] = low[main_rows:]
+        if j % 2 == 1:
+            row = iota((main_rows, extra_rows), 0)
+            want = (row // ROWS) * extra + (row % ROWS) // pieces
+            pick = (iota((main_rows, extra_rows), 1) == want).astype(F32).astype(BF16)
+            rowp = iota((main_rows, pair_piece), 0) % pieces
+            tail = jnp.zeros((main_rows, pair_piece), F32)
+            for p in range(pieces):
+                tail = jnp.where(rowp == p, mm(pick, fr[:, p * pair_piece:(p + 1) * pair_piece]), tail)
+            f2[m, pair, :, :, pair_w:] = tail.astype(BF16).reshape(blocks, ROWS, pair_piece)
+            local(("f", m, pair), f2.at[m, pair, c * experts + z], ret.at[m, z, c, pair])
+            for t in range(1, blocks):
+                to = (ex + t) % blocks
+                remote(
+                    ("f", m, pair, t), f2.at[m, pair, (to % 2) * experts + to // 2],
+                    ret.at[m, z, c, pair], (d, to),
+                )
+        return jnp.sum(jnp.sum(total * total, axis=0, keepdims=True), axis=1, keepdims=True)
+
+    def unpack(m):
+        _, idc, _, slot_c = place[m]
+        col = iota((toks, slots), 1)
+        pick = ((idc == col // ROWS) & (slot_c == col % ROWS)).astype(F32).astype(BF16)
+        pick_x = (idc == col // ROWS) & (slot_c == ROWS + (col % ROWS) // pieces)
+        for pair in range(CHUNKS // 2):
+            locals_[("f", m, pair)].wait()
+            for t in range(1, blocks):
+                frm = (ex + blocks - t) % blocks
+                arrived(("f", m, pair, t), ret.at[m, frm // 2, frm % 2, pair])
+        for h in range(2):
+            for pair in range(CHUNKS // 2):
+                for p in range(pieces):
+                    at = p * pair_piece
+                    main = ret[m, :, h, pair, :, at:at + pair_piece].reshape(slots, pair_piece)
+                    tails = ret[m, :, h, pair, :, pair_w:].reshape(slots, pair_piece)
+                    pick_p = (pick_x & (col % pieces == p)).astype(F32).astype(BF16)
+                    value = mm(pick, main) + mm(pick_p, tails)
+                    base = h * half + pair * pair_w + at
+                    out_ref[m, :, base:base + pair_piece] = value.astype(BF16)
+
+    def clip(total, count):
+        return jnp.minimum(1.0, clip_target / jnp.sqrt((total + width) / (width * (count + 1.0))))
+
+    pack(0)
+    pl.semaphore_wait(barrier, ndev - 1)
+    dispatch(0)
+    pack(1)
+    dispatch(1)
+
+    def spread_stats(buf, me, peers, ssems, rsems, dev_of):
+        def one(t, carry):
+            pltpu.make_async_remote_copy(
+                src_ref=buf.at[me], dst_ref=buf.at[me], send_sem=ssems.at[t], recv_sem=rsems.at[t],
+                device_id=dev_of((me + t) % peers), device_id_type=MESH,
+            ).start()
+            return carry
+
+        lax.fori_loop(1, peers, one, 0)
+
+    def await_stats(buf, me, peers, ssems, rsems, dev_of):
+        def one(t, carry):
+            frm = (me + peers - t) % peers
+            copy = pltpu.make_async_remote_copy(
+                src_ref=buf.at[me], dst_ref=buf.at[frm], send_sem=ssems.at[t], recv_sem=rsems.at[t],
+                device_id=dev_of((me + t) % peers), device_id_type=MESH,
+            )
+            copy.wait_recv()
+            copy.wait_send()
+            return carry
+
+        lax.fori_loop(1, peers, one, 0)
+
+    whole = (ndev, csend, crecv, lambda g: (g // ne, g % ne))
+    plane = (nd * 2, qsend, qrecv, lambda q: (q // 2, z * 2 + q % 2))
+    last = (ndev, fsend, frecv, lambda g: (g // ne, g % ne))
+
+    spread_stats(cst, flat, *whole)
+    for t in range(experts):
+        gather_own(0, t)
+    for t in range(experts):
+        gather_xy(0, t)
+    for t in range(experts):
+        gather_diag(0, t)
+    gather_end(0)
+    weights[0].wait()
+    weights[1].wait()
+    tiles = ff // LANES
+    marks = [0, (2 * tiles) // 7, (4 * tiles) // 7, (6 * tiles) // 7, tiles]
+    spread(0)
+    gate_up(0, marks[0], marks[1])
+    for t in range(experts):
+        gather_own(1, t)
+    gate_up(0, marks[1], marks[2])
+    for t in range(experts // 2):
+        gather_xy(1, t)
+    gate_up(0, marks[2], marks[4])
+    for t in range(experts // 2, experts):
+        gather_xy(1, t)
+    weights[2].wait()
+    step_a(0, 0)
+    step_a(0, 1)
+    step_b(0, 0)
+    step_a(0, 2)
+    step_b(0, 1)
+    step_a(0, 3)
+    step_b(0, 2)
+    step_b(0, 3)
+    for t in range(experts):
+        gather_diag(1, t)
+    step_c(0, 0)
+    step_c(0, 1)
+    gather_end(1)
+    spread(1)
+    gate_up(1, marks[0], marks[2])
+    step_c(0, 2)
+    step_c(0, 3)
+    squares = step_d(0, 0)
+    squares = squares + step_d(0, 1)
+    gate_up(1, marks[2], marks[4])
+    squares = squares + step_d(0, 2)
+    squares = squares + step_d(0, 3)
+    sqst[flat_q] = jnp.broadcast_to(squares, (8, LANES))
+    spread_stats(sqst, flat_q, *plane)
+    await_stats(cst, flat, *whole)
+    count_sum = jnp.sum(cst[...], axis=0)
+    await_stats(sqst, flat_q, *plane)
+    square_sum = jnp.sum(sqst[...], axis=0)[:1, :1]
+    masked = jnp.where((row8 == 0) & (lane8 == z), count_sum, 0.0)
+    count_here = jnp.sum(jnp.sum(masked, axis=0, keepdims=True), axis=1, keepdims=True)
+    scaled_hidden(clip(square_sum, count_here))
+    step_a(1, 0)
+    step_a(1, 1)
+    step_b(1, 0)
+    step_a(1, 2)
+    step_b(1, 1)
+    step_c(1, 0)
+    step_a(1, 3)
+    step_b(1, 2)
+    step_c(1, 1)
+    step_b(1, 3)
+    step_c(1, 2)
+    squares = step_d(1, 0)
+    step_c(1, 3)
+    squares = squares + step_d(1, 1)
+    unpack(0)
+    squares = squares + step_d(1, 2)
+    squares = squares + step_d(1, 3)
+    fst[flat] = jnp.where(lane8 == z, jnp.broadcast_to(squares, (8, LANES)), 0.0)
+    spread_stats(fst, flat, *last)
+    unpack(1)
+    await_stats(fst, flat, *last)
+    count_last = jnp.sum(jnp.where(row8 == micro - 1, count_sum, 0.0), axis=0, keepdims=True)
+    scale_ref[...] = clip(jnp.sum(fst[...], axis=0), count_last)
+    wait_sent(lambda key: True)
+
+
+def fused(sizes, tokens, expert_of, w_gate, w_up, w_down):
+    micro, toks, width, ff, nd, ne, cap = sizes
+    extra = cap - ROWS
+    pieces = ROWS // extra
+    piece = width // pieces
+    experts = ne // SPAN
+    blocks = experts * SPAN
+    ch = width // 2 // CHUNKS
+    wide = width + piece
+    pair_wide = 2 * ch + 2 * ch // pieces
+    rows = nd * blocks * cap
+    one = blocks * cap
+    ndev = nd * ne
+    dma = pltpu.SemaphoreType.DMA
+    vmem = pl.BlockSpec(memory_space=pltpu.VMEM)
+    anyw = pl.BlockSpec(memory_space=pl.ANY)
+    out, scale = pl.pallas_call(
+        functools.partial(kernel, sizes),
+        out_shape=(
+            jax.ShapeDtypeStruct((micro, toks, width), BF16),
+            jax.ShapeDtypeStruct((8, LANES), F32),
+        ),
+        in_specs=[vmem, vmem, vmem, anyw, anyw, anyw],
+        out_specs=(vmem, vmem),
+        scratch_shapes=[
+            pltpu.VMEM((width, ff), BF16),
+            pltpu.VMEM((width, ff), BF16),
+            pltpu.VMEM((ff, width), BF16),
+            pltpu.VMEM((micro, experts, ROWS, wide), BF16),
+            pltpu.VMEM((micro, nd, blocks, ROWS, wide), BF16),
+            pltpu.VMEM((nd * blocks * extra, width), BF16),
+            pltpu.VMEM((rows, ff), BF16),
+            pltpu.VMEM((rows, ff), F32),
+            pltpu.VMEM((rows, ff), F32),
+            pltpu.VMEM((CHUNKS, rows, ch), BF16),
+            pltpu.VMEM((micro, CHUNKS, rows, ch), BF16),
+            pltpu.VMEM((CHUNKS, nd, one, ch), BF16),
+            pltpu.VMEM((micro, CHUNKS, one, ch), BF16),
+            pltpu.VMEM((micro, CHUNKS, one, ch), BF16),
+            pltpu.VMEM((micro, CHUNKS, one, ch), BF16),
+            pltpu.VMEM((blocks * extra, 2 * ch), BF16),
+            pltpu.VMEM((micro, CHUNKS // 2, blocks, ROWS, pair_wide), BF16),
+            pltpu.VMEM((micro, experts, 2, CHUNKS // 2, ROWS, pair_wide), BF16),
+            pltpu.VMEM((ndev, 8, LANES), F32),
+            pltpu.VMEM((nd * 2, 8, LANES), F32),
+            pltpu.VMEM((ndev, 8, LANES), F32),
+            dma((3,)),
+            dma((160,)),
+            dma((160,)),
+            dma((8,)),
+            dma((ndev,)),
+            dma((ndev,)),
+            dma((nd * 2,)),
+            dma((nd * 2,)),
+            dma((ndev,)),
+            dma((ndev,)),
+        ],
+        compiler_params=pltpu.CompilerParams(
+            collective_id=0, has_side_effects=True, vmem_limit_bytes=67043328
+        ),
+    )(
+        tokens,
+        expert_of.reshape(micro, 1, toks),
+        expert_of.reshape(micro, toks, 1),
+        w_gate, w_up, w_down,
+    )
+    return out, scale[0, :experts]
+
+
+def entry(tokens, expert_of, w_gate, w_up, w_down):
+    micro, toks, width = tokens.shape
+    ff = w_gate.shape[2]
+    nd = lax.axis_size("dp")
+    ne = lax.axis_size("expert")
+    experts = ne // SPAN
+    cap = max(2, 9 * toks // (8 * experts))
+    extra = cap - ROWS
+    fits = (
+        micro == 2 and nd == 4 and experts == 4 and SPAN == 2 and extra > 0 and ROWS % extra == 0
+        and (ne * extra) % ROWS == 0 and ff % LANES == 0 and (width * extra) % (ROWS * LANES * CHUNKS) == 0
+    )
+    if not fits:
+        return body(tokens, expert_of, w_gate, w_up, w_down)
+    return fused((micro, toks, width, ff, nd, ne, cap), tokens, expert_of, w_gate, w_up, w_down)
+
+
 def solution(mesh):
     return jax.shard_map(
-        body,
+        entry,
         mesh=mesh,
         in_specs=(
             P(None, ("dp", "expert"), None),

time: 471 us -> 139 us (0.30)
  waiting for transfers between devices: 201 us -> 0 us
  blocking collectives: 160 us -> 0 us
  Pallas kernels: 0 us -> 133 us
  matrix products: 61.5 us -> 0 us
  between operations: 13.9 us -> 0.64 us
  local copies, waits for them, and re-layouts: 15 us -> 4.89 us
  starting transfers between devices: 9.35 us -> 0 us
  other arithmetic: 8.55 us -> 0 us
    pallas_call x0 -> x1, Pallas kernels: none -> 133 us  [fused(): pl.pallas_call(functools.partial(kernel, sizes), out_shape=(jax.ShapeDtyp...]
    all_to_all x2 -> x0, blocking collectives: 86.1 us -> none  [body(): lax.all_to_all(sending_all, 'expert', split_axis=0, concat_axis=0, tiled=...]
    all_to_all x2 -> x0, waiting for transfers between devices: 75.3 us -> none  [body(): lax.all_to_all(halves, 'expert', split_axis=0, concat_axis=0, tiled=True)]
    psum x2 -> x0, blocking collectives: 74.2 us -> none  [body(): lax.psum((counts_local, square_local), ('dp', 'expert'))]
    reduce_scatter x2 -> x0, waiting for transfers between devices: 70.1 us -> none  [body(): lax.psum_scatter(jnp.dot(hidden, down_local, preferred_element_type=jnp.f...]
    dot_general x9 -> x0, matrix products: 61.5 us -> none  [the longest x2 27.3 us: body(): jnp.dot(hidden, down_local, preferred_element_type=jnp.float32)]
    all_gather x2 -> x0, waiting for transfers between devices: 56 us -> none  [body(): rows_in = lax.all_gather(flat_rows, 'dp', axis=0, tiled=True)]
    reshape x8 -> x1, local copies, waits for them, and re-layouts: 10.7 us -> 1.42 us  [fused(): expert_of.reshape(micro, toks, 1)]
  transfers between devices with their start and end apart: 6 -> 0, of which waited for: 5 -> 0; matrix products, arithmetic and copies ran while one was open for 2% -> 0% of each run, Pallas kernels for 0% -> 0%
where the time goes in v1:
time: 139 us
  Pallas kernels  133 us (96%)
  local copies, waits for them, and re-layouts  4.89 us (4%)
    pallas_call x1, Pallas kernels, fused(): pl.pallas_call(functools.partial(kernel, sizes), out_shape=(jax.ShapeDtyp...  133 us

profile of v1, /device:TPU:0, one launch (start us, length us, event | category | flops | bytes accessed | tf_op | source)
XLA Modules:
  0.0 138.7 jit_solution(10979556096688521641)
XLA Ops:
  0.6 1.4 %copy.8.idc_ref = s32[2,64,1]{2,1,0:T(8,128)} copy(s32[2,64,1]{1,0,2:T(2,128)} %bitcast.6) | data formatting | bytes 1024 | tf_op jit(solution)/shard_map/reshape | solution.py:561
  2.0 133.2 %shard_map.68 = (bf16[2,64,4096]{2,1,0:T(8,128)(2,1)}, f32[8,128]{1,0:T(8,128)}) custom-call(bf16[2,64,4096]{2,1,0:T(8,128)(2,1)} %tok_ref.1, s32[2,1,64]{2,1,0:T(1,128)} %bitcast.7, s32[2,64,1]{2,1,0:T(8,128)} %copy.8.idc_ref, bf16[1,4096,896]{2,1,0:T(8,128)(2,1)} %wg_hbm.1, bf16[1,4096,896]{2,1,0:T(8,128)(2,1)} %wu_hbm.1, bf16[1,896,4096]{2,1,0:T(8,128)(2,1)} %wd_hbm.1), custom_call_target="tpu_custom_call" | custom-call | tf_op jit(solution)/shard_map/pallas_call | solution.py:514
  135.2 1.2 slice_bitcast_fusion
  136.4 2.3 %copy.10 = bf16[2,64,4096]{2,1,0:T(8,128)(2,1)} copy(bf16[2,64,4096]{2,1,0:T(8,128)(2,1)} %get-tuple-element.8) | data formatting | bytes 2097152

commit v2 on v1

--- a/solution.py
+++ b/solution.py
@@ -93,7 +93,7 @@
 
 def kernel(
     sizes,
-    tok_ref, idr_ref, idc_ref, wg_hbm, wu_hbm, wd_hbm,
+    tok_ref, idr_ref, wg_hbm, wu_hbm, wd_hbm,
     out_ref, scale_ref,
     wg, wu, wd, pk, xg, xr, hid, g1, u1, sb, rb, own, rd, ra, rc, fr, f2, ret,
     cst, sqst, fst,
@@ -146,7 +146,8 @@
     counts = []
     for m in range(micro):
         idr = idr_ref[m]
-        idc = idc_ref[m]
+        same = iota((toks, toks), 0) == iota((toks, toks), 1)
+        idc = jnp.sum(jnp.where(same, idr, 0).astype(F32), axis=1, keepdims=True).astype(jnp.int32)
         before_r = (idc == idr) & (iota((toks, toks), 0) < iota((toks, toks), 1))
         slot_r = jnp.sum(before_r.astype(F32), axis=0, keepdims=True).astype(jnp.int32)
         before_c = (idc == idr) & (iota((toks, toks), 1) < iota((toks, toks), 0))
@@ -168,10 +169,11 @@
         pick_x = ((idr == row // ROWS) & (slot_r == ROWS + (row % ROWS) // pieces)).astype(F32).astype(BF16)
         rowp = iota((slots, piece), 0) % pieces
         tail = jnp.zeros((slots, piece), F32)
+        both = jnp.concatenate([pick, pick_x], axis=0)
         for p in range(pieces):
-            cols = tok_ref[m, :, p * piece:(p + 1) * piece]
-            pk[m, :, :, p * piece:(p + 1) * piece] = mm(pick, cols).astype(BF16).reshape(experts, ROWS, piece)
-            tail = jnp.where(rowp == p, mm(pick_x, cols), tail)
+            got = mm(both, tok_ref[m, :, p * piece:(p + 1) * piece])
+            pk[m, :, :, p * piece:(p + 1) * piece] = got[:slots].astype(BF16).reshape(experts, ROWS, piece)
+            tail = jnp.where(rowp == p, got[slots:], tail)
         pk[m, :, :, width:] = tail.astype(BF16).reshape(experts, ROWS, piece)
 
     sends = []
@@ -330,6 +332,9 @@
         arrived(("rd", m, j), rd.at[m, j])
         own[j, second] = (own[j, second].astype(F32) + rd[m, j].astype(F32)).astype(BF16)
         remote(("rc", m, j), own.at[j, second], rc.at[m, j], (second, ex))
+
+    def span(j):
+        return (0, ch) if j % 2 == 0 else (ch, pair_w + pair_piece)
 
     def step_d(m, j):
         arrived(("ra", m, j), ra.at[m, j])
@@ -349,13 +354,17 @@
             for p in range(pieces):
                 tail = jnp.where(rowp == p, mm(pick, fr[:, p * pair_piece:(p + 1) * pair_piece]), tail)
             f2[m, pair, :, :, pair_w:] = tail.astype(BF16).reshape(blocks, ROWS, pair_piece)
-            local(("f", m, pair), f2.at[m, pair, c * experts + z], ret.at[m, z, c, pair])
-            for t in range(1, blocks):
-                to = (ex + t) % blocks
-                remote(
-                    ("f", m, pair, t), f2.at[m, pair, (to % 2) * experts + to // 2],
-                    ret.at[m, z, c, pair], (d, to),
-                )
+        low_col, high_col = span(j)
+        local(
+            ("f", m, j), f2.at[m, pair, c * experts + z, :, low_col:high_col],
+            ret.at[m, z, c, pair, :, low_col:high_col],
+        )
+        for t in range(1, blocks):
+            to = (ex + t) % blocks
+            remote(
+                ("f", m, j, t), f2.at[m, pair, (to % 2) * experts + to // 2, :, low_col:high_col],
+                ret.at[m, z, c, pair, :, low_col:high_col], (d, to),
+            )
         return jnp.sum(jnp.sum(total * total, axis=0, keepdims=True), axis=1, keepdims=True)
 
     def unpack(m):
@@ -363,19 +372,22 @@
         col = iota((toks, slots), 1)
         pick = ((idc == col // ROWS) & (slot_c == col % ROWS)).astype(F32).astype(BF16)
         pick_x = (idc == col // ROWS) & (slot_c == ROWS + (col % ROWS) // pieces)
-        for pair in range(CHUNKS // 2):
-            locals_[("f", m, pair)].wait()
+        picks = jnp.concatenate(
+            [(pick_x & (col % pieces == p)).astype(F32).astype(BF16) for p in range(pieces)], axis=0
+        )
+        for j in range(CHUNKS):
+            locals_[("f", m, j)].wait()
+            low, high = span(j)
             for t in range(1, blocks):
                 frm = (ex + blocks - t) % blocks
-                arrived(("f", m, pair, t), ret.at[m, frm // 2, frm % 2, pair])
+                arrived(("f", m, j, t), ret.at[m, frm // 2, frm % 2, j // 2, :, low:high])
         for h in range(2):
             for pair in range(CHUNKS // 2):
+                main = mm(pick, ret[m, :, h, pair, :, :pair_w].reshape(slots, pair_w))
+                tails = mm(picks, ret[m, :, h, pair, :, pair_w:].reshape(slots, pair_piece))
                 for p in range(pieces):
                     at = p * pair_piece
-                    main = ret[m, :, h, pair, :, at:at + pair_piece].reshape(slots, pair_piece)
-                    tails = ret[m, :, h, pair, :, pair_w:].reshape(slots, pair_piece)
-                    pick_p = (pick_x & (col % pieces == p)).astype(F32).astype(BF16)
-                    value = mm(pick, main) + mm(pick_p, tails)
+                    value = main[:, at:at + pair_piece] + tails[p * toks:(p + 1) * toks]
                     base = h * half + pair * pair_w + at
                     out_ref[m, :, base:base + pair_piece] = value.astype(BF16)
 
@@ -385,8 +397,6 @@
     pack(0)
     pl.semaphore_wait(barrier, ndev - 1)
     dispatch(0)
-    pack(1)
-    dispatch(1)
 
     def spread_stats(buf, me, peers, ssems, rsems, dev_of):
         def one(t, carry):
@@ -416,31 +426,38 @@
     last = (ndev, fsend, frecv, lambda g: (g // ne, g % ne))
 
     spread_stats(cst, flat, *whole)
-    for t in range(experts):
+    gather_own(0, 0)
+    pack(1)
+    for t in range(1, experts):
         gather_own(0, t)
-    for t in range(experts):
+        if t > 1:
+            gather_xy(0, t - 2)
+    dispatch(1)
+    for t in range(experts - 2, experts):
         gather_xy(0, t)
+    gather_own(1, 0)
     for t in range(experts):
         gather_diag(0, t)
     gather_end(0)
     weights[0].wait()
     weights[1].wait()
     tiles = ff // LANES
-    marks = [0, (2 * tiles) // 7, (4 * tiles) // 7, (6 * tiles) // 7, tiles]
+    marks = [0, (2 * tiles) // 7, (4 * tiles) // 7, tiles]
     spread(0)
+    gather_own(1, 1)
     gate_up(0, marks[0], marks[1])
-    for t in range(experts):
+    for t in range(2, experts):
         gather_own(1, t)
     gate_up(0, marks[1], marks[2])
     for t in range(experts // 2):
         gather_xy(1, t)
-    gate_up(0, marks[2], marks[4])
-    for t in range(experts // 2, experts):
-        gather_xy(1, t)
+    gate_up(0, marks[2], marks[3])
     weights[2].wait()
     step_a(0, 0)
     step_a(0, 1)
     step_b(0, 0)
+    for t in range(experts // 2, experts):
+        gather_xy(1, t)
     step_a(0, 2)
     step_b(0, 1)
     step_a(0, 3)
@@ -449,15 +466,16 @@
     for t in range(experts):
         gather_diag(1, t)
     step_c(0, 0)
-    step_c(0, 1)
     gather_end(1)
     spread(1)
-    gate_up(1, marks[0], marks[2])
+    step_c(0, 1)
+    gate_up(1, marks[0], marks[1])
     step_c(0, 2)
+    gate_up(1, marks[1], marks[2])
     step_c(0, 3)
     squares = step_d(0, 0)
     squares = squares + step_d(0, 1)
-    gate_up(1, marks[2], marks[4])
+    gate_up(1, marks[2], marks[3])
     squares = squares + step_d(0, 2)
     squares = squares + step_d(0, 3)
     sqst[flat_q] = jnp.broadcast_to(squares, (8, LANES))
@@ -517,7 +535,7 @@
             jax.ShapeDtypeStruct((micro, toks, width), BF16),
             jax.ShapeDtypeStruct((8, LANES), F32),
         ),
-        in_specs=[vmem, vmem, vmem, anyw, anyw, anyw],
+        in_specs=[vmem, vmem, anyw, anyw, anyw],
         out_specs=(vmem, vmem),
         scratch_shapes=[
             pltpu.VMEM((width, ff), BF16),
@@ -542,9 +560,9 @@
             pltpu.VMEM((nd * 2, 8, LANES), F32),
             pltpu.VMEM((ndev, 8, LANES), F32),
             dma((3,)),
-            dma((160,)),
-            dma((160,)),
-            dma((8,)),
+            dma((224,)),
+            dma((224,)),
+            dma((16,)),
             dma((ndev,)),
             dma((ndev,)),
             dma((nd * 2,)),
@@ -558,7 +576,6 @@
     )(
         tokens,
         expert_of.reshape(micro, 1, toks),
-        expert_of.reshape(micro, toks, 1),
         w_gate, w_up, w_down,
     )
     return out, scale[0, :experts]

time: 139 us -> 137 us (0.986)
  local copies, waits for them, and re-layouts: 4.89 us -> 3.48 us
    reshape x1 -> x0, local copies, waits for them, and re-layouts: 1.42 us -> none  [fused(): expert_of.reshape(micro, toks, 1)]
where the time goes in v2:
time: 137 us
  Pallas kernels  133 us (97%)
  local copies, waits for them, and re-layouts  3.48 us (3%)
    pallas_call x1, Pallas kernels, fused(): pl.pallas_call(functools.partial(kernel, sizes), out_shape=(jax.ShapeDtyp...  133 us

profile of v2, /device:TPU:0, one launch (start us, length us, event | category | flops | bytes accessed | tf_op | source)
XLA Modules:
  0.0 137.2 jit_solution(14207272073235968559)
XLA Ops:
  0.6 133.1 %shard_map.68 = (bf16[2,64,4096]{2,1,0:T(8,128)(2,1)}, f32[8,128]{1,0:T(8,128)}) custom-call(bf16[2,64,4096]{2,1,0:T(8,128)(2,1)} %tok_ref.1, s32[2,1,64]{2,1,0:T(1,128)} %bitcast.5, bf16[1,4096,896]{2,1,0:T(8,128)(2,1)} %wg_hbm.1, bf16[1,4096,896]{2,1,0:T(8,128)(2,1)} %wu_hbm.1, bf16[1,896,4096]{2,1,0:T(8,128)(2,1)} %wd_hbm.1), custom_call_target="tpu_custom_call" | custom-call | tf_op jit(solution)/shard_map/pallas_call | solution.py:532
  133.8 1.2 slice_bitcast_fusion
  134.9 2.3 %copy.9 = bf16[2,64,4096]{2,1,0:T(8,128)(2,1)} copy(bf16[2,64,4096]{2,1,0:T(8,128)(2,1)} %get-tuple-element.8) | data formatting | bytes 2097152
